TPU v7x, 128 devices: a whole 4x4x4 slice. The times are simulated.
128 devices in a mesh: req: 8 (over z, core), unit: 16 (over x, y).
Axes of the slice: x: 4, y: 4, z: 4, core: 2. Of those that a mesh axis runs over, the one named last changes fastest.
Arguments:
- tokens: bfloat16 [128, 384, 1536], P('req'), may hold values from -6 to 6
- lengths: int32 [128], P('req'), may hold values from 1 to 384, 30720 in all
- gate_proj: float32 [1536, 3072], P(('req', 'unit')), may hold values from -0.15625 to 0.15625
- input_proj: float32 [1536, 3072], P(('req', 'unit')), may hold values from -0.15625 to 0.15625
- state_proj: float32 [1536, 256], P(('req', 'unit')), may hold values from -0.15625 to 0.15625
- step_proj: float32 [1536, 48], P(('req', 'unit')), may hold values from -0.15625 to 0.15625
- out_proj: float32 [1536, 3072], P(('req', 'unit')), may hold values from -0.109375 to 0.109375
- conv_weight: float32 [4, 3328], replicated, may hold values from -3 to 3
- step_bias: float32 [48], replicated, may hold values from -4 to -1
- log_rate: float32 [48], replicated, may hold values from -3.5 to 0
- skip_gain: float32 [48], replicated, may hold values from 0.5 to 3
- norm_gain: float32 [3072], replicated, may hold values from 0.1 to 1.9
Outputs:
- mixed: bfloat16 [128, 384, 1536], P(('req', 'unit'))
- final_state: float32 [128, 48, 64, 128], P(('req', 'unit'))
All inputs are finite; a program needn't handle non-finite values. No bound on the sum of `lengths` on one device may be relied on, other than what follows from the above.
Results may differ from a plain program's by a relative error of at most 0.0084.
Values may be sent and summed in bfloat16 or wider, within the bound.
No kernel may reach another device: no remote copies, remote signals or barrier semaphores. Data moves between devices by JAX's collectives and lax.ppermute only.
A program may use at most 192 MiB of HBM per device.

v0:
```python
import jax
import jax.numpy as jnp
from jax import lax
from jax.sharding import PartitionSpec as P

SPAN = 128
EPSILON = 1e-05
HIGHEST = lax.Precision.HIGHEST


def causal_conv(values, kernel):
    kernel_len = kernel.shape[0]
    seq_len = values.shape[-2]
    axis_time = values.ndim - 2
    padding = [(0, 0)] * axis_time + [(kernel_len - 1, 0), (0, 0)]
    padded = jnp.pad(values.astype(jnp.float32), padding)
    running = jnp.zeros(values.shape, jnp.float32)
    for offset in range(kernel_len):
        running = running + kernel[offset] * lax.slice_in_dim(
            padded, offset, offset + seq_len, axis=axis_time
        )
    return jax.nn.silu(running)


def ssd_scan(head_in, step_size, b_matrix, c_matrix, rate_per, skip_gain, block_len):
    req_count, seq_len, head_count, head_dim = head_in.shape
    state_dim = b_matrix.shape[-1]
    blocks = seq_len // block_len
    b_short = b_matrix.astype(jnp.bfloat16)
    c_short = c_matrix.astype(jnp.bfloat16)
    b_wide = lax.optimization_barrier(b_short).astype(jnp.float32)
    c_wide = lax.optimization_barrier(c_short).astype(jnp.float32)
    shaped_x = jnp.moveaxis(
        head_in.reshape(req_count, blocks, block_len, head_count, head_dim), 1, 0
    )
    shaped_dt = jnp.moveaxis(step_size.reshape(req_count, blocks, block_len, head_count), 1, 0)
    shaped_bs = jnp.moveaxis(b_short.reshape(req_count, blocks, block_len, state_dim), 1, 0)
    shaped_cs = jnp.moveaxis(c_short.reshape(req_count, blocks, block_len, state_dim), 1, 0)
    shaped_b = jnp.moveaxis(b_wide.reshape(req_count, blocks, block_len, state_dim), 1, 0)
    shaped_c = jnp.moveaxis(c_wide.reshape(req_count, blocks, block_len, state_dim), 1, 0)
    decays = jnp.cumsum(shaped_dt * rate_per, axis=2)
    where_lower = jnp.arange(block_len)[:, None] >= jnp.arange(block_len)[None, :]

    def advance(carried, pieces):
        piece_x, piece_dt, piece_bs, piece_cs, piece_b, piece_c, piece_log = pieces
        intersection = jnp.einsum(
            "rtn,rsn->rts", piece_cs, piece_bs, preferred_element_type=jnp.float32
        )
        log_gaps = piece_log[:, :, None, :] - piece_log[:, None, :, :]
        factor = jnp.exp(jnp.where(where_lower[None, :, :, None], log_gaps, -jnp.inf))
        mixing = intersection[..., None] * factor * piece_dt[:, None, :, :]
        inside = jnp.einsum("rtsh,rshp->rthp", mixing, piece_x, precision=HIGHEST)
        earlier = (
            jnp.einsum("rtn,rhpn->rthp", piece_c, carried, precision=HIGHEST)
            * jnp.exp(piece_log)[..., None]
        )
        ending = piece_log[:, -1, :]
        weight_in = jnp.exp(ending[:, None, :] - piece_log) * piece_dt
        fresh_state = jnp.einsum(
            "rsh,rshp,rsn->rhpn", weight_in, piece_x, piece_b, precision=HIGHEST
        )
        carried = jnp.exp(ending)[:, :, None, None] * carried + fresh_state
        return (carried, inside + earlier)

    start_state = jnp.zeros((req_count, head_count, head_dim, state_dim), jnp.float32)
    final_state, outputs = lax.scan(
        advance,
        start_state,
        (shaped_x, shaped_dt, shaped_bs, shaped_cs, shaped_b, shaped_c, decays),
    )
    scanned = jnp.moveaxis(outputs, 0, 1).reshape(req_count, seq_len, head_count, head_dim)
    return (scanned + skip_gain[:, None] * head_in, final_state)


def body(
    tokens,
    lengths,
    gate_proj,
    input_proj,
    state_proj,
    step_proj,
    out_proj,
    conv_weight,
    step_bias,
    log_rate,
    skip_gain,
    norm_gain,
):
    unit_count = lax.axis_size("unit")
    unit_id = lax.axis_index("unit")
    group_reqs, seq_len, model_dim = tokens.shape
    own_reqs = group_reqs // unit_count
    inner_dim = gate_proj.shape[1]
    head_count = log_rate.shape[0]
    head_dim = inner_dim // head_count
    state_dim = state_proj.shape[1] // 2
    flat_tokens = tokens.reshape(group_reqs * seq_len, model_dim)
    rate_per = -jnp.exp(log_rate)
    position = jnp.arange(seq_len)
    moved = (
        lax.all_to_all(
            gate_proj.astype(jnp.bfloat16), "unit", split_axis=1, concat_axis=0, tiled=True
        ),
        lax.all_to_all(
            input_proj.astype(jnp.bfloat16), "unit", split_axis=1, concat_axis=0, tiled=True
        ),
        lax.all_to_all(
            state_proj.astype(jnp.bfloat16), "unit", split_axis=1, concat_axis=0, tiled=True
        ),
        lax.all_to_all(
            step_proj.astype(jnp.bfloat16), "unit", split_axis=1, concat_axis=0, tiled=True
        ),
        lax.all_to_all(
            out_proj.astype(jnp.bfloat16), "unit", split_axis=1, concat_axis=0, tiled=True
        ),
    )
    pieces = (
        lax.all_gather(moved[0], "req", axis=0, tiled=True),
        lax.all_gather(moved[1], "req", axis=0, tiled=True),
        lax.all_gather(moved[2], "req", axis=0, tiled=True),
        lax.all_gather(moved[3], "req", axis=0, tiled=True),
        lax.all_gather(moved[4], "req", axis=0, tiled=True),
    )
    projected = tuple(
        (
            jnp.dot(flat_tokens, weight_piece, preferred_element_type=jnp.float32)
            for weight_piece in pieces[:4]
        )
    )
    out_piece = pieces[4]
    gate_sum, input_sum, state_sum, step_sum, out_block = projected + (out_piece,)

    def as_cols(summed):
        return summed.astype(jnp.bfloat16).reshape(group_reqs, seq_len, summed.shape[1])

    gate_cols = as_cols(gate_sum)
    input_cols = as_cols(input_sum)
    state_cols = as_cols(state_sum)
    step_cols = as_cols(step_sum)
    own_len = lax.dynamic_slice_in_dim(lengths, unit_id * own_reqs, own_reqs, 0)
    own_live = (position[None, :] < own_len[:, None]).astype(jnp.float32)
    gate_all, input_all, state_all, step_all = (
        lax.all_to_all(gate_cols, "unit", split_axis=0, concat_axis=2, tiled=True),
        lax.all_to_all(input_cols, "unit", split_axis=0, concat_axis=2, tiled=True),
        lax.all_to_all(state_cols, "unit", split_axis=0, concat_axis=2, tiled=True),
        lax.all_to_all(step_cols, "unit", split_axis=0, concat_axis=2, tiled=True),
    )
    x_conv = causal_conv(input_all, conv_weight[:, :inner_dim])
    s_conv = causal_conv(state_all, conv_weight[:, inner_dim:])
    step_size = jax.nn.softplus(step_all.astype(jnp.float32) + step_bias) * own_live[..., None]
    scanned, final_state = ssd_scan(
        x_conv.reshape(own_reqs, seq_len, head_count, head_dim),
        step_size,
        s_conv[..., :state_dim],
        s_conv[..., state_dim:],
        rate_per,
        skip_gain,
        SPAN,
    )
    gated = scanned.reshape(own_reqs, seq_len, inner_dim) * jax.nn.silu(
        gate_all.astype(jnp.float32)
    )
    spread = jnp.mean(gated * gated, axis=-1, keepdims=True)
    normed = (gated * lax.rsqrt(spread + EPSILON) * norm_gain).astype(jnp.bfloat16)
    returned = lax.all_to_all(normed, "unit", split_axis=2, concat_axis=0, tiled=True)
    mixed = lax.psum_scatter(
        jnp.einsum("rse,de->rsd", returned, out_block, preferred_element_type=jnp.float32),
        "unit",
        scatter_dimension=0,
        tiled=True,
    )
    mixed_out = (mixed * own_live[..., None]).astype(jnp.bfloat16)
    return (mixed_out, final_state)


def solution(mesh):
    placed = (
        P("req", None, None),
        P("req"),
        P(("req", "unit"), None),
        P(("req", "unit"), None),
        P(("req", "unit"), None),
        P(("req", "unit"), None),
        P(("req", "unit"), None),
        P(),
        P(),
        P(),
        P(),
        P(),
    )
    return jax.shard_map(
        body,
        mesh=mesh,
        in_specs=placed,
        out_specs=(P(("req", "unit"), None, None), P(("req", "unit"), None, None, None)),
        check_vma=False,
    )
```

profile of v0, /device:TPU:1, one launch (start us, length us, event | category | flops | bytes accessed | tf_op | source)
XLA Modules:
  0.0 799.4 jit_solution(10832921844835051563)
XLA Ops:
  8.6 7.6 all-to-all-start
  16.2 1.0 fusion.66
  18.0 1.2 dynamic_slice.28
  20.5 0.9 convert_element_type.157
  23.8 0.9 convert_element_type.169
  26.4 0.9 convert_element_type.176
  28.2 6.7 all-to-all-start.4
  34.9 14.1 %all-gather = bf16[8,192,3]{1,2,0:T(4,128)(2,1)S(1)} all-gather(bf16[1,192,3]{1,2,0:T(4,128)(2,1)S(1)} %reshape.481), channel_id=1, replica_groups=mesh['req'=8,'unit'=16] {'req'}, dimensions={0}, use_global_device_ids=true | all-gather | bytes 10368 | tf_op jit(solution)/shard_map/all_gather | solution.py:121
  49.1 12.0 %convolution_convert_fusion.3 = bf16[6144,3]{0,1:T(4,128)(2,1)} fusion(bf16[6144,1536]{1,0:T(8,128)(2,1)} %bitcast.188, bf16[1536,3]{0,1:T(4,128)(2,1)S(1)} %reshape.482), kind=kOutput, calls=%fused_computation.50 | convolution fusion | flops 56641536 | bytes 18920448 | tf_op jit(solution)/shard_map/dot_general | solution.py:126
  61.1 6.9 all-to-all-start.1
  68.2 13.0 %all-gather.1 = bf16[8,192,16]{1,2,0:T(8,128)(2,1)S(1)} all-gather(bf16[1,192,16]{1,2,0:T(8,128)(2,1)S(1)} %reshape.483), channel_id=1, replica_groups=mesh['req'=8,'unit'=16] {'req'}, dimensions={0}, use_global_device_ids=true | all-gather | bytes 55296 | tf_op jit(solution)/shard_map/all_gather | solution.py:120
  81.4 11.3 %convolution_convert_fusion.2 = bf16[6144,16]{0,1:T(8,128)(2,1)S(1)} fusion(bf16[6144,1536]{1,0:T(8,128)(2,1)} %bitcast.189, bf16[1536,16]{0,1:T(8,128)(2,1)S(1)} %reshape.484), kind=kOutput, calls=%fused_computation.49 | convolution fusion | flops 302088192 | bytes 19120128 | tf_op jit(solution)/shard_map/dot_general | solution.py:126
  93.4 6.9 all-to-all-start.2
  101.8 5.3 all-to-all-done.2
  107.1 3.6 all-to-all-start.6
  110.7 14.9 %all_gather.16 = bf16[1536,192]{1,0:T(8,128)(2,1)S(1)} all-gather(bf16[192,192]{1,0:T(8,128)(2,1)S(1)} %all_to_all.119), channel_id=1, replica_groups=mesh['req'=8,'unit'=16] {'req'}, dimensions={0}, use_global_device_ids=true | all-gather | bytes 663552 | tf_op jit(solution)/shard_map/all_gather | solution.py:119
  125.6 6.9 all-to-all-start.5
  132.6 10.6 %convolution_convert_fusion.1 = bf16[6144,192]{0,1:T(8,128)(2,1)S(1)} fusion(bf16[6144,1536]{1,0:T(8,128)(2,1)} %bitcast.190, bf16[1536,192]{1,0:T(8,128)(2,1)S(1)} %all_gather.16), kind=kOutput, calls=%fused_computation.45 | convolution fusion | flops 3625058304 | bytes 21823488 | tf_op jit(solution)/shard_map/dot_general | solution.py:126
  143.2 1.8 copy.162
  145.1 6.9 all-to-all-start.3
  152.0 14.2 %all_gather.18 = bf16[1536,192]{1,0:T(8,128)(2,1)S(1)} all-gather(bf16[192,192]{1,0:T(8,128)(2,1)S(1)} %all_to_all.129), channel_id=1, replica_groups=mesh['req'=8,'unit'=16] {'req'}, dimensions={0}, use_global_device_ids=true | all-gather | bytes 663552 | tf_op jit(solution)/shard_map/all_gather | solution.py:118
  166.2 10.6 %convolution_convert_fusion = bf16[6144,192]{0,1:T(8,128)(2,1)S(1)} fusion(bf16[6144,1536]{1,0:T(8,128)(2,1)} %bitcast.191, bf16[1536,192]{1,0:T(8,128)(2,1)S(1)} %all_gather.18), kind=kOutput, calls=%fused_computation.44 | convolution fusion | flops 3625058304 | bytes 21823488 | tf_op jit(solution)/shard_map/dot_general | solution.py:126
  176.8 1.8 copy.161
  181.6 2.0 all-to-all-done.3
  183.6 4.9 all-to-all-start.7
  188.5 2.1 bitcast_convert_fusion
  190.7 2.1 copy-done.1
  192.8 6.9 divide_multiply_fusion
  199.6 8.0 transpose_reshape_reshape.3
  207.6 173.0 %while.13 = (s32[]{:T(128)}, f32[1,48,64,128]{3,2,1,0:T(8,128)S(1)}, f32[3,1,128,48,64]{2,0,4,3,1:T(4,128)}, f32[3,1,128,48]{2,3,1,0:T(8,128)S(1)}, f32[3,1,128,...) while((s32[]{:T(128)}, ...), condition=%wide.region_2.3_spmd.clone, body=%wide.region_1.2_spmd.clone.sunk | while | flops 1822060544 | bytes 19582040 | solution.py:66
  207.6 2.3 fusion.97
  210.0 4.5 constant_dynamic-slice_fusion.4
  215.3 0.9 constant_dynamic-slice_fusion.5
  216.3 7.4 bitcast_add_fusion.5
  223.7 39.1 %dynamic_update_slice.6 = f32[3,1,128,48,64]{2,0,4,3,1:T(4,128)} dynamic-update-slice(f32[3,1,128,48,64]{2,0,4,3,1:T(4,128)} %get-tuple-element.262, f32[1,1,128,48,64]{2,0,4,3,1:T(1,128)} %bitcast.194, s32[]{:T(128)} %get-tuple-element.260, s32[]{:T(128)} %constant.43.clone.1..sunk, s32[]{:T(128)} %constant.43.clone.1..sunk, s32[]{:T(128)} %constant.43.clone.1..sunk, s32[]{:T(128)} %constant.43.clone.1..sunk) | dynamic-update-slice | bytes 3145732 | tf_op jit(solution)/shard_map/while/body/jit(dynamic_update_index_in_dim)/dynamic_update_slice | solution.py:66
  263.1 2.2 bitcast_add_fusion.4
  265.3 2.3 fusion.97
  267.6 4.5 constant_dynamic-slice_fusion.4
  272.1 0.9 fusion.98
  273.0 0.9 constant_dynamic-slice_fusion.5
  274.0 7.4 bitcast_add_fusion.5
  281.3 39.1 %dynamic_update_slice.6 = f32[3,1,128,48,64]{2,0,4,3,1:T(4,128)} dynamic-update-slice(f32[3,1,128,48,64]{2,0,4,3,1:T(4,128)} %get-tuple-element.262, f32[1,1,128,48,64]{2,0,4,3,1:T(1,128)} %bitcast.194, s32[]{:T(128)} %get-tuple-element.260, s32[]{:T(128)} %constant.43.clone.1..sunk, s32[]{:T(128)} %constant.43.clone.1..sunk, s32[]{:T(128)} %constant.43.clone.1..sunk, s32[]{:T(128)} %constant.43.clone.1..sunk) | dynamic-update-slice | bytes 3145732 | tf_op jit(solution)/shard_map/while/body/jit(dynamic_update_index_in_dim)/dynamic_update_slice | solution.py:66
  320.7 2.2 bitcast_add_fusion.4
  323.0 2.3 fusion.97
  325.3 4.5 constant_dynamic-slice_fusion.4
  329.8 0.9 fusion.98
  330.7 0.9 constant_dynamic-slice_fusion.5
  331.6 7.4 bitcast_add_fusion.5
  339.0 39.1 %dynamic_update_slice.6 = f32[3,1,128,48,64]{2,0,4,3,1:T(4,128)} dynamic-update-slice(f32[3,1,128,48,64]{2,0,4,3,1:T(4,128)} %get-tuple-element.262, f32[1,1,128,48,64]{2,0,4,3,1:T(1,128)} %bitcast.194, s32[]{:T(128)} %get-tuple-element.260, s32[]{:T(128)} %constant.43.clone.1..sunk, s32[]{:T(128)} %constant.43.clone.1..sunk, s32[]{:T(128)} %constant.43.clone.1..sunk, s32[]{:T(128)} %constant.43.clone.1..sunk) | dynamic-update-slice | bytes 3145732 | tf_op jit(solution)/shard_map/while/body/jit(dynamic_update_index_in_dim)/dynamic_update_slice | solution.py:66
  378.4 2.2 bitcast_add_fusion.4
  380.6 9.1 %reshape_transpose.3 = f32[1,384,3072]{1,2,0:T(8,128)} reshape(f32[3,1,128,48,64]{2,0,4,3,1:T(4,128)} %get-tuple-element.60) | data formatting | bytes 9437184 | tf_op jit(solution)/shard_map/reshape;transpose | solution.py:71
  389.7 6.8 all-to-all-start.9
  396.5 15.3 %multiply_reduce_fusion = (f32[384]{0:T(512)S(1)}, f32[1,384,3072]{1,2,0:T(8,128)S(1)}) fusion(bf16[16,384,192]{1,2,0:T(8,128)(2,1)} %all-to-all-done.7, f32[1,384,3072]{1,2,0:T(8,128)} %reshape_transpose.3, f32[3072]{0:T(1024)S(1)} %mul.288, f32[1,384,3072]{1,2,0:T(8,128)} %bitcast.193, f32[3072]{0:T(1024)S(1)} %bitcast.216, f32[3072]{0:T(1024)S(1)} %bitcast.218, ...), kind=kLoop, calls=%fused_computation.64 | loop fusion | flops 24772224 | bytes 16578048 | tf_op jit(solution)/shard_map/reduce_sum | solution.py:163
  412.4 44.7 %copy.164 = bf16[1,384,3072]{1,0,2:T(2,128)(2,1)} copy(bf16[1,384,3072]{1,2,0:T(8,128)(2,1)S(1)} %multiply_convert_fusion) | data formatting | bytes 4718592 | tf_op jit(solution)/shard_map/convert_element_type | solution.py:164
  457.6 50.9 %reduce.4 = bf16[3072,384]{1,0:T(8,128)(2,1)S(1)} reduce(bf16[3072,1,384]{2,1,0:T(2,128)(2,1)} %bitcast.195, bf16[]{:T(256)} %broadcast.240), dimensions={1}, to_apply=%bitcast.159.reduce_sub_computation | reduce | bytes 4718594
  508.4 2.2 reshape.500
  510.6 6.8 all-to-all-start.8
  517.5 16.9 %all_gather.19 = bf16[1536,192]{1,0:T(8,128)(2,1)S(1)} all-gather(bf16[192,192]{1,0:T(8,128)(2,1)S(1)} %all_to_all.138), channel_id=1, replica_groups=mesh['req'=8,'unit'=16] {'req'}, dimensions={0}, use_global_device_ids=true | all-gather | bytes 663552 | tf_op jit(solution)/shard_map/all_gather | solution.py:122
  534.4 10.7 %all-to-all-done.8 = bf16[16,2,36864]{2,1,0:T(2,128)(2,1)S(1)} async-done(((bf16[16,2,36864]{2,1,0:T(2,128)(2,1)}), bf16[16,2,36864]{2,1,0:T(2,128)(2,1)S(1)}, u32[]{:S(2)}, u32[]{:S(2)}) %all-to-all-start.8) | async-done | bytes 2359328 | tf_op jit(solution)/shard_map/all_to_all | solution.py:165
  545.1 6.9 reshape.501
  552.1 2.7 copy.147
  554.8 14.9 %fusion.50 = f32[16,384,1536]{2,1,0:T(8,128)} fusion(bf16[16,384,192]{1,2,0:T(8,128)(2,1)S(1)} %bitcast.197, bf16[1536,192]{1,0:T(8,128)(2,1)S(1)} %all_gather.19), kind=kOutput, calls=%fused_computation.70 | convolution fusion | flops 3623878656 | bytes 40697856 | tf_op jit(solution)/shard_map/rse,de->rsd/dot_general | solution.py:167
  570.3 219.0 %reduce-scatter.4.cloned.1.call-done = f32[1,384,1536]{2,1,0:T(8,128)} async-done(((f32[16,384,1536]{2,1,0:T(8,128)}), f32[1,384,1536]{2,1,0:T(8,128)}) %reduce-scatter.4.cloned.1.call-update) | async-done | bytes 2359312
  789.3 2.9 multiply_convert_fusion.1
  (83 shorter events, 17.5 us)
Async XLA Ops:
  8.6 19.6 %all-to-all-start = ((bf16[12,16,3]{0,2,1:T(4,128)(2,1)}), bf16[12,16,3]{0,2,1:T(4,128)(2,1)S(1)}, u32[]{:S(2)}, u32[]{:S(2)}) async-start(bf16[12,16,3]{0,2,1:T(4,128)(2,1)} %all_to_all.111), calls=%async_computation | async-start | bytes 32768 | tf_op jit(solution)/shard_map/all_to_all | solution.py:110
  28.2 32.9 %all-to-all-start.4 = ((bf16[12,16,16]{0,2,1:T(8,128)(2,1)}), bf16[12,16,16]{0,2,1:T(8,128)(2,1)S(1)}, u32[]{:S(2)}, u32[]{:S(2)}) async-start(bf16[12,16,16]{0,2,1:T(8,128)(2,1)} %bitcast.17), calls=%async_computation.4 | async-start | bytes 131072 | tf_op jit(solution)/shard_map/all_to_all | solution.py:107
  61.1 32.3 %all-to-all-start.1 = ((bf16[16,384,3]{1,2,0:T(4,128)(2,1)}), bf16[16,384,3]{1,2,0:T(4,128)(2,1)S(1)}, u32[]{:S(2)}, u32[]{:S(2)}) async-start(bf16[16,384,3]{1,2,0:T(4,128)(2,1)} %bitcast.2), calls=%async_computation.1 | async-start | bytes 98304 | tf_op jit(solution)/shard_map/all_to_all | solution.py:146
  81.4 19.1 %copy-start.3 = (f32[48]{0:T(128)S(1)}, f32[48]{0:T(128)}, u32[]{:S(2)}) copy-start(f32[48]{0:T(128)} %param.22) | copy-start | bytes 580
  93.4 13.7 %all-to-all-start.2 = ((bf16[12,16,192]{2,0,1:T(8,128)(2,1)}), bf16[12,16,192]{2,0,1:T(8,128)(2,1)S(1)}, u32[]{:S(2)}, u32[]{:S(2)}) async-start(bf16[12,16,192]{2,0,1:T(8,128)(2,1)} %copy.121), calls=%async_computation.2 | async-start | bytes 262144 | tf_op jit(solution)/shard_map/all_to_all | solution.py:104
  107.1 18.5 %all-to-all-start.6 = ((bf16[12,16,192]{2,0,1:T(8,128)(2,1)}), bf16[12,16,192]{2,0,1:T(8,128)(2,1)S(1)}, u32[]{:S(2)}, u32[]{:S(2)}) async-start(bf16[12,16,192]{2,0,1:T(8,128)(2,1)} %copy.139), calls=%async_computation.6 | async-start | bytes 262144 | tf_op jit(solution)/shard_map/all_to_all | solution.py:101
  125.6 19.4 %all-to-all-start.5 = ((bf16[16,384,16]{1,2,0:T(8,128)(2,1)}), bf16[16,384,16]{1,2,0:T(8,128)(2,1)S(1)}, u32[]{:S(2)}, u32[]{:S(2)}) async-start(bf16[16,384,16]{1,2,0:T(8,128)(2,1)} %bitcast.158), calls=%async_computation.5 | async-start | bytes 393216 | tf_op jit(solution)/shard_map/all_to_all | solution.py:145
  145.1 38.5 %all-to-all-start.3 = ((bf16[16,384,192]{1,2,0:T(8,128)(2,1)}), bf16[16,384,192]{1,2,0:T(8,128)(2,1)}, u32[]{:S(2)}, u32[]{:S(2)}) async-start(bf16[16,384,192]{1,2,0:T(8,128)(2,1)} %bitcast.199), calls=%async_computation.3 | async-start | bytes 4718592 | tf_op jit(solution)/shard_map/all_to_all | solution.py:144
  183.6 206.1 %all-to-all-start.7 = ((bf16[16,384,192]{1,2,0:T(8,128)(2,1)}), bf16[16,384,192]{1,2,0:T(8,128)(2,1)}, u32[]{:S(2)}, u32[]{:S(2)}) async-start(bf16[16,384,192]{1,2,0:T(8,128)(2,1)} %bitcast.198), calls=%async_computation.7 | async-start | bytes 4718592 | tf_op jit(solution)/shard_map/all_to_all | solution.py:143
  190.7 2.1 copy-start.1
  380.6 9.1 %copy-start = (f32[1,48,64,128]{3,2,1,0:T(8,128)}, f32[1,48,64,128]{3,2,1,0:T(8,128)S(1)}, u32[]{:S(2)}) copy-start(f32[1,48,64,128]{3,2,1,0:T(8,128)S(1)} %get-tuple-element.59) | copy-start | bytes 4718596
  389.7 120.9 %all-to-all-start.9 = ((bf16[12,16,192]{2,0,1:T(8,128)(2,1)}), bf16[12,16,192]{2,0,1:T(8,128)(2,1)S(1)}, u32[]{:S(2)}, u32[]{:S(2)}) async-start(bf16[12,16,192]{2,0,1:T(8,128)(2,1)} %copy.142), calls=%async_computation.9 | async-start | bytes 262144 | tf_op jit(solution)/shard_map/all_to_all | solution.py:113
  396.5 15.3 %copy-start.2 = (f32[3072]{0:T(1024)S(1)}, f32[3072]{0:T(1024)}, u32[]{:S(2)}) copy-start(f32[3072]{0:T(1024)} %param.25) | copy-start | bytes 36868
  510.6 34.5 %all-to-all-start.8 = ((bf16[16,2,36864]{2,1,0:T(2,128)(2,1)}), bf16[16,2,36864]{2,1,0:T(2,128)(2,1)S(1)}, u32[]{:S(2)}, u32[]{:S(2)}) async-start(bf16[16,2,36864]{2,1,0:T(2,128)(2,1)} %reshape.500), calls=%async_computation.8 | async-start | bytes 4718592 | tf_op jit(solution)/shard_map/all_to_all | solution.py:165
  517.4 271.9 %reduce-scatter.4.cloned.1.call-start = ((), (), s32[]{:S(2)}) async-start(), calls=%async_computation.11 | async-start | bytes 40108032
Sparse Core Ops, SparseCore 0:
  569.9 219.3 reduce-scatter.3
where the time goes:
time: 813 us; the launch traced here: 799 us
  waiting for transfers between devices  237 us (29%)
  local copies, waits for them, and re-layouts  226 us (28%)
  matrix products  97.7 us (12%)
  other arithmetic  86.6 us (11%)
  blocking collectives  73.2 us (9%)
  starting transfers between devices  64 us (8%)
  between operations  14.8 us (2%)
    unnamed x2, waiting for transfers between devices  219 us
    dynamic_update_slice x3, local copies, waits for them, and re-layouts, ssd_scan(): lax.scan(advance, start_state, (shaped_x, shaped_dt, shaped_bs, shaped_cs...  117 us
    unnamed x2, other arithmetic  50.9 us
    convert_element_type x1, local copies, waits for them, and re-layouts, body(): (gated * lax.rsqrt(spread + EPSILON) * norm_gain).astype(jnp.bfloat16)  44.7 us
    dot_general x4, matrix products, body(): jnp.dot(flat_tokens, weight_piece, preferred_element_type=jnp.float32)  44.5 us
    dot_general x3, matrix products, advance(): inside = jnp.einsum('rtsh,rshp->rthp', mixing, piece_x, precision=HIGHEST)  22.1 us
    all_gather x1, blocking collectives, body(): lax.all_gather(moved[4], 'req', axis=0, tiled=True)  16.9 us
  transfers between devices with their start and end apart: 11, of which 4 were waited for; matrix products, arithmetic and copies ran while one was open for 47% of the time, Pallas kernels for 0%

commit v1 on v0

--- a/solution.py
+++ b/solution.py
@@ -6,6 +6,19 @@
 SPAN = 128
 EPSILON = 1e-05
 HIGHEST = lax.Precision.HIGHEST
+
+
+def ring_gather(array, axis, dim):
+    ways = lax.axis_size(axis)
+    up = [(d, (d + 1) % ways) for d in range(ways)]
+    down = [(d, (d - 1) % ways) for d in range(ways)]
+    earlier, later = ([array], [array])
+    for _ in range(ways // 2):
+        earlier.append(lax.ppermute(earlier[-1], axis, up))
+    for _ in range((ways - 1) // 2):
+        later.append(lax.ppermute(later[-1], axis, down))
+    line = jnp.concatenate([*earlier[::-1], *later[1:]], axis=dim)
+    return jnp.roll(line, (lax.axis_index(axis) - ways // 2) * array.shape[dim], axis=dim)
 
 
 def causal_conv(values, kernel):
@@ -119,7 +132,7 @@
         lax.all_gather(moved[1], "req", axis=0, tiled=True),
         lax.all_gather(moved[2], "req", axis=0, tiled=True),
         lax.all_gather(moved[3], "req", axis=0, tiled=True),
-        lax.all_gather(moved[4], "req", axis=0, tiled=True),
+        ring_gather(moved[4], "req", 0),
     )
     projected = tuple(
         (

time: 813 us -> 821 us (level)
  blocking collectives: 73.2 us -> 56.3 us
  starting transfers between devices: 64 us -> 76 us
    all_gather x1 -> x0, blocking collectives: 16.9 us -> none  [body(): lax.all_gather(moved[4], 'req', axis=0, tiled=True)]
    ppermute x0 -> x7, starting transfers between devices: none -> 12 us  [the longest x4 10.5 us: ring_gather(): earlier.append(lax.ppermute(earlier[-1], axis, up))]
  transfers between devices with their start and end apart: 11 -> 18, of which waited for: 4 -> 11; matrix products, arithmetic and copies ran while one was open for 47% -> 47% of each run, Pallas kernels for 0% -> 0%
where the time goes in v1:
time: 821 us; the launch traced here: 807 us
  waiting for transfers between devices  241 us (29%)
  local copies, waits for them, and re-layouts  233 us (28%)
  matrix products  97.8 us (12%)
  other arithmetic  88.1 us (11%)
  starting transfers between devices  76 us (9%)
  blocking collectives  56.3 us (7%)
  between operations  14.8 us (2%)
    unnamed x2, waiting for transfers between devices  219 us
    dynamic_update_slice x3, local copies, waits for them, and re-layouts, ssd_scan(): lax.scan(advance, start_state, (shaped_x, shaped_dt, shaped_bs, shaped_cs...  117 us
    unnamed x2, other arithmetic  52.3 us
    convert_element_type x1, local copies, waits for them, and re-layouts, body(): (gated * lax.rsqrt(spread + EPSILON) * norm_gain).astype(jnp.bfloat16)  44.7 us
    dot_general x4, matrix products, body(): jnp.dot(flat_tokens, weight_piece, preferred_element_type=jnp.float32)  44.5 us
    dot_general x3, matrix products, advance(): inside = jnp.einsum('rtsh,rshp->rthp', mixing, piece_x, precision=HIGHEST)  22.1 us
    unnamed x18, local copies, waits for them, and re-layouts  20.7 us
  transfers between devices with their start and end apart: 18, of which 11 were waited for; matrix products, arithmetic and copies ran while one was open for 47% of the time, Pallas kernels for 0%

profile of v1, /device:TPU:1, one launch (start us, length us, event | category | flops | bytes accessed | tf_op | source)
XLA Modules:
  0.0 807.0 jit_solution(7225951996586752394)
XLA Ops:
  8.6 7.6 all-to-all-start
  16.2 1.0 fusion.68
  18.0 1.2 dynamic_slice.32
  28.2 6.7 all-to-all-start.4
  35.0 14.1 %all-gather = bf16[8,192,3]{1,2,0:T(4,128)(2,1)S(1)} all-gather(bf16[1,192,3]{1,2,0:T(4,128)(2,1)S(1)} %reshape.481), channel_id=1, replica_groups=mesh['req'=8,'unit'=16] {'req'}, dimensions={0}, use_global_device_ids=true | all-gather | bytes 10368 | tf_op jit(solution)/shard_map/all_gather | solution.py:134
  49.2 12.0 %convolution_convert_fusion.3 = bf16[6144,3]{0,1:T(4,128)(2,1)} fusion(bf16[6144,1536]{1,0:T(8,128)(2,1)} %bitcast.188, bf16[1536,3]{0,1:T(4,128)(2,1)S(1)} %reshape.482), kind=kOutput, calls=%fused_computation.50 | convolution fusion | flops 56641536 | bytes 18920448 | tf_op jit(solution)/shard_map/dot_general | solution.py:139
  61.1 6.9 all-to-all-start.1
  68.2 13.0 %all-gather.1 = bf16[8,192,16]{1,2,0:T(8,128)(2,1)S(1)} all-gather(bf16[1,192,16]{1,2,0:T(8,128)(2,1)S(1)} %reshape.483), channel_id=1, replica_groups=mesh['req'=8,'unit'=16] {'req'}, dimensions={0}, use_global_device_ids=true | all-gather | bytes 55296 | tf_op jit(solution)/shard_map/all_gather | solution.py:133
  81.4 11.3 %convolution_convert_fusion.2 = bf16[6144,16]{0,1:T(8,128)(2,1)S(1)} fusion(bf16[6144,1536]{1,0:T(8,128)(2,1)} %bitcast.189, bf16[1536,16]{0,1:T(8,128)(2,1)S(1)} %reshape.484), kind=kOutput, calls=%fused_computation.49 | convolution fusion | flops 302088192 | bytes 19120128 | tf_op jit(solution)/shard_map/dot_general | solution.py:139
  93.5 6.9 all-to-all-start.2
  101.9 5.3 all-to-all-done.2
  107.1 3.6 all-to-all-start.6
  110.8 14.9 %all_gather.13 = bf16[1536,192]{1,0:T(8,128)(2,1)S(1)} all-gather(bf16[192,192]{1,0:T(8,128)(2,1)S(1)} %all_to_all.119), channel_id=1, replica_groups=mesh['req'=8,'unit'=16] {'req'}, dimensions={0}, use_global_device_ids=true | all-gather | bytes 663552 | tf_op jit(solution)/shard_map/all_gather | solution.py:132
  125.7 6.9 all-to-all-start.5
  132.6 10.6 %convolution_convert_fusion.1 = bf16[6144,192]{0,1:T(8,128)(2,1)S(1)} fusion(bf16[6144,1536]{1,0:T(8,128)(2,1)} %bitcast.190, bf16[1536,192]{1,0:T(8,128)(2,1)S(1)} %all_gather.13), kind=kOutput, calls=%fused_computation.45 | convolution fusion | flops 3625058304 | bytes 21823488 | tf_op jit(solution)/shard_map/dot_general | solution.py:139
  143.2 1.8 copy.182
  145.1 6.9 all-to-all-start.3
  152.0 14.2 %all_gather.15 = bf16[1536,192]{1,0:T(8,128)(2,1)S(1)} all-gather(bf16[192,192]{1,0:T(8,128)(2,1)S(1)} %all_to_all.129), channel_id=1, replica_groups=mesh['req'=8,'unit'=16] {'req'}, dimensions={0}, use_global_device_ids=true | all-gather | bytes 663552 | tf_op jit(solution)/shard_map/all_gather | solution.py:131
  166.2 10.6 %convolution_convert_fusion = bf16[6144,192]{0,1:T(8,128)(2,1)S(1)} fusion(bf16[6144,1536]{1,0:T(8,128)(2,1)} %bitcast.191, bf16[1536,192]{1,0:T(8,128)(2,1)S(1)} %all_gather.15), kind=kOutput, calls=%fused_computation.44 | convolution fusion | flops 3625058304 | bytes 21823488 | tf_op jit(solution)/shard_map/dot_general | solution.py:139
  176.8 1.8 copy.181
  181.6 2.0 all-to-all-done.3
  183.6 4.9 all-to-all-start.7
  188.6 2.1 bitcast_convert_fusion
  190.7 2.1 copy-done.1
  192.8 6.9 divide_multiply_fusion
  199.7 8.0 transpose_reshape_reshape.3
  207.7 173.0 %while.13 = (s32[]{:T(128)}, f32[1,48,64,128]{3,2,1,0:T(8,128)S(1)}, f32[3,1,128,48,64]{2,0,4,3,1:T(4,128)}, f32[3,1,128,48]{2,3,1,0:T(8,128)S(1)}, f32[3,1,128,...) while((s32[]{:T(128)}, ...), condition=%wide.region_2.3_spmd.clone, body=%wide.region_1.2_spmd.clone.sunk | while | flops 1822060544 | bytes 19582040 | solution.py:79
  207.7 2.3 fusion.99
  210.0 4.5 constant_dynamic-slice_fusion.4
  216.4 7.4 bitcast_add_fusion.5
  223.7 39.1 %dynamic_update_slice.6 = f32[3,1,128,48,64]{2,0,4,3,1:T(4,128)} dynamic-update-slice(f32[3,1,128,48,64]{2,0,4,3,1:T(4,128)} %get-tuple-element.262, f32[1,1,128,48,64]{2,0,4,3,1:T(1,128)} %bitcast.194, s32[]{:T(128)} %get-tuple-element.260, s32[]{:T(128)} %constant.65.clone.1..sunk, s32[]{:T(128)} %constant.65.clone.1..sunk, s32[]{:T(128)} %constant.65.clone.1..sunk, s32[]{:T(128)} %constant.65.clone.1..sunk) | dynamic-update-slice | bytes 3145732 | tf_op jit(solution)/shard_map/while/body/jit(dynamic_update_index_in_dim)/dynamic_update_slice | solution.py:79
  263.1 2.2 bitcast_add_fusion.4
  265.4 2.3 fusion.99
  267.7 4.5 constant_dynamic-slice_fusion.4
  274.0 7.4 bitcast_add_fusion.5
  281.4 39.1 %dynamic_update_slice.6 = f32[3,1,128,48,64]{2,0,4,3,1:T(4,128)} dynamic-update-slice(f32[3,1,128,48,64]{2,0,4,3,1:T(4,128)} %get-tuple-element.262, f32[1,1,128,48,64]{2,0,4,3,1:T(1,128)} %bitcast.194, s32[]{:T(128)} %get-tuple-element.260, s32[]{:T(128)} %constant.65.clone.1..sunk, s32[]{:T(128)} %constant.65.clone.1..sunk, s32[]{:T(128)} %constant.65.clone.1..sunk, s32[]{:T(128)} %constant.65.clone.1..sunk) | dynamic-update-slice | bytes 3145732 | tf_op jit(solution)/shard_map/while/body/jit(dynamic_update_index_in_dim)/dynamic_update_slice | solution.py:79
  320.8 2.2 bitcast_add_fusion.4
  323.0 2.3 fusion.99
  325.4 4.5 constant_dynamic-slice_fusion.4
  331.7 7.4 bitcast_add_fusion.5
  339.1 39.1 %dynamic_update_slice.6 = f32[3,1,128,48,64]{2,0,4,3,1:T(4,128)} dynamic-update-slice(f32[3,1,128,48,64]{2,0,4,3,1:T(4,128)} %get-tuple-element.262, f32[1,1,128,48,64]{2,0,4,3,1:T(1,128)} %bitcast.194, s32[]{:T(128)} %get-tuple-element.260, s32[]{:T(128)} %constant.65.clone.1..sunk, s32[]{:T(128)} %constant.65.clone.1..sunk, s32[]{:T(128)} %constant.65.clone.1..sunk, s32[]{:T(128)} %constant.65.clone.1..sunk) | dynamic-update-slice | bytes 3145732 | tf_op jit(solution)/shard_map/while/body/jit(dynamic_update_index_in_dim)/dynamic_update_slice | solution.py:79
  378.5 2.2 bitcast_add_fusion.4
  380.7 9.1 %reshape_transpose.3 = f32[1,384,3072]{1,2,0:T(8,128)} reshape(f32[3,1,128,48,64]{2,0,4,3,1:T(4,128)} %get-tuple-element.60) | data formatting | bytes 9437184 | tf_op jit(solution)/shard_map/reshape;transpose | solution.py:84
  389.8 6.8 all-to-all-start.9
  396.7 15.4 %multiply_reduce_fusion = (f32[384]{0:T(512)S(1)}, f32[1,384,3072]{1,2,0:T(8,128)S(1)}) fusion(bf16[16,384,192]{1,2,0:T(8,128)(2,1)} %all-to-all-done.7, f32[1,384,3072]{1,2,0:T(8,128)} %reshape_transpose.3, f32[3072]{0:T(1024)S(1)} %mul.291, f32[1,384,3072]{1,2,0:T(8,128)} %bitcast.193, f32[3072]{0:T(1024)S(1)} %bitcast.216, f32[3072]{0:T(1024)S(1)} %bitcast.218, ...), kind=kLoop, calls=%fused_computation.64 | loop fusion | flops 24772224 | bytes 16578048 | tf_op jit(solution)/shard_map/reduce_sum | solution.py:176
  412.6 44.7 %copy.184 = bf16[1,384,3072]{1,0,2:T(2,128)(2,1)} copy(bf16[1,384,3072]{1,2,0:T(8,128)(2,1)S(1)} %multiply_convert_fusion) | data formatting | bytes 4718592 | tf_op jit(solution)/shard_map/convert_element_type | solution.py:177
  457.8 52.3 %reduce.4 = bf16[3072,384]{1,0:T(8,128)(2,1)} reduce(bf16[3072,1,384]{2,1,0:T(2,128)(2,1)} %bitcast.195, bf16[]{:T(256)} %broadcast.240), dimensions={1}, to_apply=%bitcast.159.reduce_sub_computation | reduce | bytes 4718594
  510.1 4.2 reshape.500
  514.2 6.8 all-to-all-start.8
  521.3 4.2 collective-permute-start
  525.5 1.6 collective-permute-done
  527.1 2.4 collective-permute-start.1
  530.1 1.1 collective-permute-done.1
  531.2 2.4 collective-permute-start.2
  534.4 1.3 collective-permute-start.6
  536.1 1.5 collective-permute-start.3
  537.6 1.2 collective-permute-done.6
  538.8 2.6 collective-permute-done.3
  542.2 6.7 all-to-all-done.8
  548.8 10.7 %reshape.501 = bf16[3072,1,384]{2,1,0:T(2,128)(2,1)} reshape(bf16[16,2,36864]{2,1,0:T(2,128)(2,1)} %all-to-all-done.8) | data formatting | bytes 4718592
  559.5 2.7 copy.167
  562.2 15.0 %fusion.50 = f32[16,384,1536]{2,1,0:T(8,128)} fusion(bf16[16,384,192]{1,2,0:T(8,128)(2,1)S(1)} %bitcast.197, bf16[3072,192]{0,1:T(8,128)(2,1)S(1)} %concatenate.6, s32[]{:T(128)S(6)} %select_n.44), kind=kOutput, calls=%fused_computation.73 | convolution fusion | flops 3623878656 | bytes 40697860 | tf_op jit(solution)/shard_map/rse,de->rsd/dot_general | solution.py:180
  577.8 219.0 %reduce-scatter.4.cloned.1.call-done = f32[1,384,1536]{2,1,0:T(8,128)} async-done(((f32[16,384,1536]{2,1,0:T(8,128)}), f32[1,384,1536]{2,1,0:T(8,128)}) %reduce-scatter.4.cloned.1.call-update) | async-done | bytes 2359312
  796.9 2.9 multiply_convert_fusion.1
  (98 shorter events, 27.8 us)
Async XLA Ops:
  8.6 19.6 %all-to-all-start = ((bf16[12,16,3]{0,2,1:T(4,128)(2,1)}), bf16[12,16,3]{0,2,1:T(4,128)(2,1)S(1)}, u32[]{:S(2)}, u32[]{:S(2)}) async-start(bf16[12,16,3]{0,2,1:T(4,128)(2,1)} %all_to_all.111), calls=%async_computation | async-start | bytes 32768 | tf_op jit(solution)/shard_map/all_to_all | solution.py:123
  28.2 32.9 %all-to-all-start.4 = ((bf16[12,16,16]{0,2,1:T(8,128)(2,1)}), bf16[12,16,16]{0,2,1:T(8,128)(2,1)S(1)}, u32[]{:S(2)}, u32[]{:S(2)}) async-start(bf16[12,16,16]{0,2,1:T(8,128)(2,1)} %bitcast.17), calls=%async_computation.4 | async-start | bytes 131072 | tf_op jit(solution)/shard_map/all_to_all | solution.py:120
  61.1 32.3 %all-to-all-start.1 = ((bf16[16,384,3]{1,2,0:T(4,128)(2,1)}), bf16[16,384,3]{1,2,0:T(4,128)(2,1)S(1)}, u32[]{:S(2)}, u32[]{:S(2)}) async-start(bf16[16,384,3]{1,2,0:T(4,128)(2,1)} %bitcast.2), calls=%async_computation.1 | async-start | bytes 98304 | tf_op jit(solution)/shard_map/all_to_all | solution.py:159
  81.4 19.1 %copy-start.3 = (f32[48]{0:T(128)S(1)}, f32[48]{0:T(128)}, u32[]{:S(2)}) copy-start(f32[48]{0:T(128)} %param.22) | copy-start | bytes 580
  93.5 13.7 %all-to-all-start.2 = ((bf16[12,16,192]{2,0,1:T(8,128)(2,1)}), bf16[12,16,192]{2,0,1:T(8,128)(2,1)S(1)}, u32[]{:S(2)}, u32[]{:S(2)}) async-start(bf16[12,16,192]{2,0,1:T(8,128)(2,1)} %copy.137), calls=%async_computation.2 | async-start | bytes 262144 | tf_op jit(solution)/shard_map/all_to_all | solution.py:117
  107.1 18.5 %all-to-all-start.6 = ((bf16[12,16,192]{2,0,1:T(8,128)(2,1)}), bf16[12,16,192]{2,0,1:T(8,128)(2,1)S(1)}, u32[]{:S(2)}, u32[]{:S(2)}) async-start(bf16[12,16,192]{2,0,1:T(8,128)(2,1)} %copy.155), calls=%async_computation.6 | async-start | bytes 262144 | tf_op jit(solution)/shard_map/all_to_all | solution.py:114
  125.7 19.4 %all-to-all-start.5 = ((bf16[16,384,16]{1,2,0:T(8,128)(2,1)}), bf16[16,384,16]{1,2,0:T(8,128)(2,1)S(1)}, u32[]{:S(2)}, u32[]{:S(2)}) async-start(bf16[16,384,16]{1,2,0:T(8,128)(2,1)} %bitcast.158), calls=%async_computation.5 | async-start | bytes 393216 | tf_op jit(solution)/shard_map/all_to_all | solution.py:158
  145.1 38.5 %all-to-all-start.3 = ((bf16[16,384,192]{1,2,0:T(8,128)(2,1)}), bf16[16,384,192]{1,2,0:T(8,128)(2,1)}, u32[]{:S(2)}, u32[]{:S(2)}) async-start(bf16[16,384,192]{1,2,0:T(8,128)(2,1)} %bitcast.199), calls=%async_computation.3 | async-start | bytes 4718592 | tf_op jit(solution)/shard_map/all_to_all | solution.py:157
  183.6 206.2 %all-to-all-start.7 = ((bf16[16,384,192]{1,2,0:T(8,128)(2,1)}), bf16[16,384,192]{1,2,0:T(8,128)(2,1)}, u32[]{:S(2)}, u32[]{:S(2)}) async-start(bf16[16,384,192]{1,2,0:T(8,128)(2,1)} %bitcast.198), calls=%async_computation.7 | async-start | bytes 4718592 | tf_op jit(solution)/shard_map/all_to_all | solution.py:156
  190.7 2.1 copy-start.1
  380.7 9.1 %copy-start = (f32[1,48,64,128]{3,2,1,0:T(8,128)}, f32[1,48,64,128]{3,2,1,0:T(8,128)S(1)}, u32[]{:S(2)}) copy-start(f32[1,48,64,128]{3,2,1,0:T(8,128)S(1)} %get-tuple-element.59) | copy-start | bytes 4718596
  389.8 124.4 %all-to-all-start.9 = ((bf16[12,16,192]{2,0,1:T(8,128)(2,1)}), bf16[12,16,192]{2,0,1:T(8,128)(2,1)S(1)}, u32[]{:S(2)}, u32[]{:S(2)}) async-start(bf16[12,16,192]{2,0,1:T(8,128)(2,1)} %copy.158), calls=%async_computation.9 | async-start | bytes 262144 | tf_op jit(solution)/shard_map/all_to_all | solution.py:126
  396.7 15.4 %copy-start.2 = (f32[3072]{0:T(1024)S(1)}, f32[3072]{0:T(1024)}, u32[]{:S(2)}) copy-start(f32[3072]{0:T(1024)} %param.25) | copy-start | bytes 36868
  514.2 34.6 %all-to-all-start.8 = ((bf16[16,2,36864]{2,1,0:T(2,128)(2,1)}), bf16[16,2,36864]{2,1,0:T(2,128)(2,1)}, u32[]{:S(2)}, u32[]{:S(2)}) async-start(bf16[16,2,36864]{2,1,0:T(2,128)(2,1)} %reshape.500), calls=%async_computation.8 | async-start | bytes 4718592 | tf_op jit(solution)/shard_map/all_to_all | solution.py:178
  521.1 275.8 %reduce-scatter.4.cloned.1.call-start = ((), (), s32[]{:S(2)}) async-start(), calls=%async_computation.11 | async-start | bytes 40108032
  521.3 5.9 collective-permute-start
  525.5 4.4 collective-permute-start.4
  527.1 4.0 collective-permute-start.1
  529.9 4.4 collective-permute-start.5
  531.2 5.0 collective-permute-start.2
  534.4 4.4 collective-permute-start.6
  536.1 5.3 collective-permute-start.3
Sparse Core Ops, SparseCore 0:
  577.4 219.4 reduce-scatter.3
